TPU v7x, 128 devices: a whole 4x4x4 slice. The times are simulated.
128 devices in a mesh: patch: 32 (over z, x, core), feat: 4 (over y).
Axes of the slice: x: 4, y: 4, z: 4, core: 2. Of those that a mesh axis runs over, the one named last changes fastest.
Arguments:
- node_latents: bfloat16 [16384, 512], P('patch'), may hold values from -6 to 6
- edge_latents: bfloat16 [131072, 512], P('patch'), may hold values from -6 to 6
- send_rows: int32 [32, 32, 128], P('patch'), may hold values from 0 to 511, as said below
- edge_slot: int32 [131072], P('patch'), may hold values from 0 to 4095, as said below
- receivers: int32 [131072], P('patch'), may hold values from 0 to 511
- edge_in_w: bfloat16 [3, 3, 512, 512], P(None, None, None, 'feat'), may hold values from -0.15625 to 0.15625
- edge_in_b: float32 [3, 512], P(None, 'feat'), may hold values from -3 to 3
- edge_out_w: bfloat16 [3, 512, 512], P(None, 'feat'), may hold values from -0.25 to 0.25
- edge_gain: float32 [3, 512], replicated, may hold values from 0.5 to 2
- node_in_w: bfloat16 [3, 2, 512, 512], P(None, None, None, 'feat'), may hold values from -0.1875 to 0.1875
- node_in_b: float32 [3, 512], P(None, 'feat'), may hold values from -3 to 3
- node_out_w: bfloat16 [3, 512, 512], P(None, 'feat'), may hold values from -0.25 to 0.25
- node_gain: float32 [3, 512], replicated, may hold values from 0.5 to 2
Outputs:
- node_state: bfloat16 [16384, 512], P('patch')
- edge_state: bfloat16 [131072, 512], P('patch')
Inputs may be any that keep to these rules, and one draw needn't show every extreme that they name: `send_rows`: the rows that one pair (s, d) names at slots used by some edge are distinct; unused slots hold 0. Every edge of patch d names a used slot of some patch s. Each patch names its last node row in the first slot it provides to itself. `edge_slot`: every patch holds exactly 4096 edges, all ending at its own nodes.
All inputs are finite; a program needn't handle non-finite values.
Results may differ from a plain program's by a relative error of at most 0.023.
Values may be sent and summed in bfloat16 or wider, within the bound.
No kernel may reach another device: no remote copies, remote signals or barrier semaphores. Data moves between devices by JAX's collectives and lax.ppermute only.
A program may use at most 128 MiB of HBM per device.

v0:
```python
import jax
import jax.numpy as jnp
from jax import lax
from jax.sharding import PartitionSpec as P

LAYERS = 3


def layer_norm(values, scales):
    center = values - jnp.mean(values, axis=-1, keepdims=True)
    spread = jnp.mean(center * center, axis=-1, keepdims=True)
    return center * lax.rsqrt(spread + 1e-05) * scales


def body(
    node_latents,
    edge_latents,
    send_rows,
    edge_slot,
    receivers,
    edge_in_w,
    edge_in_b,
    edge_out_w,
    edge_gain,
    node_in_w,
    node_in_b,
    node_out_w,
    node_gain,
):
    node_rows = node_latents.shape[0]
    slot_width = send_rows.shape[2]
    out_rows = send_rows[0]
    members = jnp.arange(node_rows, dtype=jnp.int32)
    remote_rows = lax.all_to_all(out_rows, "patch", split_axis=0, concat_axis=0, tiled=True)
    senders = edge_slot // slot_width * node_rows + remote_rows.reshape(-1)[edge_slot]
    incidence = (members[:, None] == receivers[None, :]).astype(jnp.bfloat16)
    edge_state = edge_latents
    node_state = node_latents
    for layer_idx in range(LAYERS):
        sender_proj = jnp.dot(
            node_state, edge_in_w[layer_idx, 1], preferred_element_type=jnp.float32
        ).astype(jnp.bfloat16)
        every_proj = lax.all_gather(sender_proj, "patch", axis=0, tiled=True)
        fetched = every_proj[senders]
        receiver_proj = jnp.dot(
            node_state, edge_in_w[layer_idx, 2], preferred_element_type=jnp.float32
        ).astype(jnp.bfloat16)
        preact = jnp.dot(edge_state, edge_in_w[layer_idx, 0], preferred_element_type=jnp.float32)
        preact = (
            preact
            + fetched.astype(jnp.float32)
            + receiver_proj[receivers].astype(jnp.float32)
            + edge_in_b[layer_idx]
        )
        edge_hidden = jax.nn.silu(preact).astype(jnp.bfloat16)
        edge_term = jnp.dot(edge_hidden, edge_out_w[layer_idx], preferred_element_type=jnp.float32)
        edge_total = lax.psum(edge_term.astype(jnp.bfloat16), "feat").astype(jnp.float32)
        message = layer_norm(edge_total, edge_gain[layer_idx])
        update = message.astype(jnp.bfloat16)
        edge_next = (edge_state.astype(jnp.float32) + message).astype(jnp.bfloat16)
        incoming = jnp.dot(incidence, update, preferred_element_type=jnp.float32).astype(
            jnp.bfloat16
        )
        node_pre = jnp.dot(node_state, node_in_w[layer_idx, 0], preferred_element_type=jnp.float32)
        node_pre = (
            node_pre
            + jnp.dot(incoming, node_in_w[layer_idx, 1], preferred_element_type=jnp.float32)
            + node_in_b[layer_idx]
        )
        node_hidden = jax.nn.silu(node_pre).astype(jnp.bfloat16)
        node_term = jnp.dot(node_hidden, node_out_w[layer_idx], preferred_element_type=jnp.float32)
        node_total = lax.psum(node_term.astype(jnp.bfloat16), "feat").astype(jnp.float32)
        node_change = layer_norm(node_total, node_gain[layer_idx])
        node_state = (node_state.astype(jnp.float32) + node_change).astype(jnp.bfloat16)
        edge_state = edge_next
    return (node_state, edge_state)


def solution(mesh):
    in_specs = (
        P("patch", None),
        P("patch", None),
        P("patch", None, None),
        P("patch"),
        P("patch"),
        P(None, None, None, "feat"),
        P(None, "feat"),
        P(None, "feat", None),
        P(),
        P(None, None, None, "feat"),
        P(None, "feat"),
        P(None, "feat", None),
        P(),
    )
    out_specs = (P("patch", None), P("patch", None))
    return jax.shard_map(body, mesh=mesh, in_specs=in_specs, out_specs=out_specs, check_vma=False)
```

profile of v0, /device:TPU:0, one launch (start us, length us, event | category | flops | bytes accessed | tf_op | source)
XLA Modules:
  0.0 679.3 jit_solution(13226365927270650812)
XLA Ops:
  7.2 2.0 convolution_convert_fusion.11
  9.2 8.3 %all-to-all-start = ((s32[32,1,128]{2,1,0:T(1,128)}), s32[32,1,128]{2,1,0:T(1,128)S(1)}, u32[]{:S(2)}, u32[]{:S(2)}) async-start(s32[32,1,128]{2,1,0:T(1,128)} %bitcast.101), calls=%async_computation | async-start | bytes 32768 | tf_op jit(solution)/shard_map/all_to_all | solution.py:34
  17.6 0.7 fusion.147
  18.3 0.7 fusion.149
  19.0 1.4 convolution_convert_fusion.10
  20.4 0.8 slice_bitcast_fusion.1
  21.2 12.1 %gather_fusion.2 = bf16[4096,128]{1,0:T(8,128)(2,1)S(1)} fusion(bf16[512,128]{1,0:T(8,128)(2,1)S(1)} %convolution_convert_fusion.10, s32[4096]{0:T(1024)S(1)} %fusion.149), kind=kCustom, calls=%fused_computation.2 | custom fusion | bytes 2113536 | tf_op jit(solution)/shard_map/gather | solution.py:52
  33.4 23.0 %gather_fusion = s32[4096]{0:T(1024)S(1)} fusion(s32[4096]{0:T(1024)S(1)} %bitcast.100, s32[4096]{0:T(1024)S(1)} %fusion.147), kind=kCustom, calls=%fused_computation | custom fusion | bytes 49152 | tf_op jit(solution)/shard_map/gather | solution.py:35
  56.4 3.1 all-gather.4.cloned.1.call-done
  59.5 13.8 %gather_fusion.1 = bf16[4096,128]{1,0:T(8,128)(2,1)S(1)} fusion(bf16[16384,128]{1,0:T(8,128)(2,1)} %all-gather.4.cloned.1.call-done, s32[4096]{0:T(1024)S(1)} %fusion.148), kind=kCustom, calls=%fused_computation.1 | custom fusion | bytes 2113536 | tf_op jit(solution)/shard_map/gather | solution.py:44
  73.3 6.6 convolution_convert_fusion.2
  79.9 0.0 all-reduce.9.cloned.1.call-start
  80.0 0.6 copy-done.9
  80.6 0.4 copy-done.3
  81.0 1.2 fusion.118
  82.2 90.0 %all-reduce.7.cloned.1.call-done = bf16[4096,512]{1,0:T(8,128)(2,1)} async-done(((bf16[4096,512]{1,0:T(8,128)(2,1)}), bf16[4096,512]{1,0:T(8,128)(2,1)}) %all-reduce.7.cloned.1.call-update) | async-done | bytes 4194320 | tf_op jit(solution)/shard_map/psum | solution.py:57
  172.2 3.0 convert_reduce_fusion.2
  175.2 0.5 copy-done
  175.7 1.8 fusion.16
  177.5 5.1 multiply_convert_fusion.5
  182.6 2.0 convolution_convert_fusion.5
  184.6 0.0 all-gather.6.cloned.1.call-start
  184.6 43.0 %all-reduce.9.cloned.1.call-done = bf16[512,512]{1,0:T(8,128)(2,1)} async-done(((bf16[512,512]{1,0:T(8,128)(2,1)}), bf16[512,512]{1,0:T(8,128)(2,1)}) %all-reduce.9.cloned.1.call-update) | async-done | bytes 524304 | tf_op jit(solution)/shard_map/psum | solution.py:72
  227.6 1.2 convert_reduce_fusion.5
  228.8 1.3 fusion.77
  230.2 1.3 fusion.80
  231.5 1.9 convolution_convert_fusion.9
  233.4 0.2 all-reduce.11.cloned.1.call-start
  233.6 1.2 convolution_convert_fusion.8
  234.8 12.1 %gather_fusion.4 = bf16[4096,128]{1,0:T(8,128)(2,1)S(1)} fusion(bf16[512,128]{1,0:T(8,128)(2,1)S(1)} %convolution_convert_fusion.8, s32[4096]{0:T(1024)S(1)} %fusion.149), kind=kCustom, calls=%fused_computation.4 | custom fusion | bytes 2113536 | tf_op jit(solution)/shard_map/gather | solution.py:52
  247.0 33.4 %all-gather.6.cloned.1.call-done = bf16[16384,128]{1,0:T(8,128)(2,1)} async-done(((bf16[512,128]{1,0:T(8,128)(2,1)}), bf16[16384,128]{1,0:T(8,128)(2,1)}) %all-gather.6.cloned.1.call-update) | async-done | bytes 4194320 | tf_op jit(solution)/shard_map/all_gather | solution.py:43
  280.3 13.8 %gather_fusion.3 = bf16[4096,128]{1,0:T(8,128)(2,1)S(1)} fusion(bf16[16384,128]{1,0:T(8,128)(2,1)} %all-gather.6.cloned.1.call-done, s32[4096]{0:T(1024)S(1)} %fusion.148), kind=kCustom, calls=%fused_computation.3 | custom fusion | bytes 2113536 | tf_op jit(solution)/shard_map/gather | solution.py:44
  294.1 7.5 %convolution_convert_fusion.1 = bf16[4096,512]{1,0:T(8,128)(2,1)} fusion(bf16[4096,128]{1,0:T(8,128)(2,1)S(1)} %gather_fusion.4, bf16[4096,128]{1,0:T(8,128)(2,1)S(1)} %gather_fusion.3, f32[128]{0:T(128)S(1)} %get-tuple-element.13, bf16[3,128,512]{2,1,0:T(8,128)(2,1)} %param.20, bf16[3,3,512,128]{3,2,1,0:T(8,128)(2,1)} %param.18, ...), kind=kOutput, calls=%fused_computation.39 | convolution fusion | flops 1095761920 | bytes 14977536 | tf_op jit(solution)/shard_map/dot_general | solution.py:56
  301.6 1.2 fusion.109
  302.8 91.0 %all-reduce.11.cloned.1.call-done = bf16[4096,512]{1,0:T(8,128)(2,1)} async-done(((bf16[4096,512]{1,0:T(8,128)(2,1)}), bf16[4096,512]{1,0:T(8,128)(2,1)}) %all-reduce.11.cloned.1.call-update) | async-done | bytes 4194320 | tf_op jit(solution)/shard_map/psum | solution.py:57
  393.8 3.0 convert_reduce_fusion.1
  396.8 0.5 copy-done.1
  397.2 1.8 fusion.11
  399.0 5.1 multiply_convert_fusion.4
  404.2 1.1 convolution_convert_fusion.4
  405.3 43.0 %all-reduce.13.cloned.1.call-done = bf16[512,512]{1,0:T(8,128)(2,1)} async-done(((bf16[512,512]{1,0:T(8,128)(2,1)}), bf16[512,512]{1,0:T(8,128)(2,1)}) %all-reduce.13.cloned.1.call-update) | async-done | bytes 524304 | tf_op jit(solution)/shard_map/psum | solution.py:72
  448.3 1.2 convert_reduce_fusion.4
  449.5 1.3 fusion.73
  450.9 1.3 fusion.76
  452.2 1.9 convolution_convert_fusion.7
  454.1 0.3 all-reduce.15.cloned.1.call-start
  454.4 8.3 %fusion.15 = bf16[4096,512]{1,0:T(8,128)(2,1)} fusion(bf16[4096,512]{1,0:T(8,128)(2,1)} %all-reduce.11.cloned.1.call-done, f32[512]{0:T(512)S(1)} %bitcast.107, f32[4096]{0:T(1024)S(1)} %add_rsqrt_fusion.1, f32[4096]{0:T(1024)S(1)} %broadcast_multiply_fusion.1, f32[512]{0:T(512)S(1)} %bitcast.105, f32[4096]{0:T(1024)S(1)} %add_rsqrt_fusion.2, ...), kind=kLoop, calls=%fused_computation.28 | loop fusion | flops 29360128 | bytes 16846848 | tf_op jit(solution)/shard_map/convert_element_type | solution.py:60
  462.7 1.2 convolution_convert_fusion.6
  463.9 12.1 %gather_fusion.6 = bf16[4096,128]{1,0:T(8,128)(2,1)S(1)} fusion(bf16[512,128]{1,0:T(8,128)(2,1)S(1)} %convolution_convert_fusion.6, s32[4096]{0:T(1024)S(1)} %fusion.149), kind=kCustom, calls=%fused_computation.6 | custom fusion | bytes 2113536 | tf_op jit(solution)/shard_map/gather | solution.py:52
  476.0 25.0 %all-gather.8.cloned.1.call-done = bf16[16384,128]{1,0:T(8,128)(2,1)} async-done(((bf16[512,128]{1,0:T(8,128)(2,1)}), bf16[16384,128]{1,0:T(8,128)(2,1)}) %all-gather.8.cloned.1.call-update) | async-done | bytes 4194320 | tf_op jit(solution)/shard_map/all_gather | solution.py:43
  501.0 13.8 %gather_fusion.5 = bf16[4096,128]{1,0:T(8,128)(2,1)S(1)} fusion(bf16[16384,128]{1,0:T(8,128)(2,1)} %all-gather.8.cloned.1.call-done, s32[4096]{0:T(1024)S(1)} %fusion.148), kind=kCustom, calls=%fused_computation.5 | custom fusion | bytes 2113536 | tf_op jit(solution)/shard_map/gather | solution.py:44
  514.8 6.6 convolution_convert_fusion
  521.4 1.2 fusion.100
  522.6 91.0 %all-reduce.15.cloned.1.call-done = bf16[4096,512]{1,0:T(8,128)(2,1)} async-done(((bf16[4096,512]{1,0:T(8,128)(2,1)}), bf16[4096,512]{1,0:T(8,128)(2,1)}) %all-reduce.15.cloned.1.call-update) | async-done | bytes 4194320 | tf_op jit(solution)/shard_map/psum | solution.py:57
  613.6 3.0 convert_reduce_fusion
  616.6 0.5 copy-done.2
  617.1 1.8 fusion.6
  618.8 5.1 multiply_convert_fusion.3
  623.9 1.1 convolution_convert_fusion.3
  625.0 5.8 fusion.10
  630.8 37.3 %all-reduce.17.cloned.1.call-done = bf16[512,512]{1,0:T(8,128)(2,1)} async-done(((bf16[512,512]{1,0:T(8,128)(2,1)}), bf16[512,512]{1,0:T(8,128)(2,1)}) %all-reduce.17.cloned.1.call-update) | async-done | bytes 524304 | tf_op jit(solution)/shard_map/psum | solution.py:72
  668.1 1.2 convert_reduce_fusion.3
  669.3 1.3 fusion.69
  670.6 2.1 fusion.72
  (46 shorter events, 0.5 us)
Async XLA Ops:
  7.2 52.3 %all-gather.4.cloned.1.call-start = ((), (), s32[]{:S(2)}) async-start(), calls=%async_computation.1 | async-start | bytes 4325376 | tf_op jit(solution)/shard_map/all_gather | solution.py:43
  9.2 24.1 %all-to-all-start = ((s32[32,1,128]{2,1,0:T(1,128)}), s32[32,1,128]{2,1,0:T(1,128)S(1)}, u32[]{:S(2)}, u32[]{:S(2)}) async-start(s32[32,1,128]{2,1,0:T(1,128)} %bitcast.101), calls=%async_computation | async-start | bytes 32768 | tf_op jit(solution)/shard_map/all_to_all | solution.py:34
  17.5 154.7 %all-reduce.7.cloned.1.call-start = ((), (), s32[]{:S(2)}) async-start(), calls=%async_computation.2 | async-start | bytes 8388608 | tf_op jit(solution)/shard_map/psum | solution.py:57
  33.3 23.1 %copy-start.5 = (s32[4096]{0:T(1024)S(1)}, s32[4096]{0:T(1024)}, u32[]{:S(2)}) copy-start(s32[4096]{0:T(1024)} %param.16) | copy-start | bytes 49156
  79.9 0.7 copy-start.9
  79.9 0.7 copy-start.7
  79.9 1.1 copy-start.3
  79.9 147.7 %all-reduce.9.cloned.1.call-start = ((), (), s32[]{:S(2)}) async-start(), calls=%async_computation.3 | async-start | bytes 1048576 | tf_op jit(solution)/shard_map/psum | solution.py:72
  82.2 95.3 %copy-start.6 = (s32[4096]{0:T(1024)S(1)}, s32[4096]{0:T(1024)}, u32[]{:S(2)}) copy-start(s32[4096]{0:T(1024)} %param.17) | copy-start | bytes 49156
  172.2 3.4 copy-start
  177.5 7.1 %copy-start.8 = (f32[3,512]{1,0:T(4,128)S(1)}, f32[3,512]{1,0:T(4,128)}, u32[]{:S(2)}) copy-start(f32[3,512]{1,0:T(4,128)} %param.25) | copy-start | bytes 18436
  184.6 95.8 %all-gather.6.cloned.1.call-start = ((), (), s32[]{:S(2)}) async-start(), calls=%async_computation.4 | async-start | bytes 4325376 | tf_op jit(solution)/shard_map/all_gather | solution.py:43
  233.4 160.4 %all-reduce.11.cloned.1.call-start = ((), (), s32[]{:S(2)}) async-start(), calls=%async_computation.5 | async-start | bytes 8388608 | tf_op jit(solution)/shard_map/psum | solution.py:57
  301.6 146.8 %all-reduce.13.cloned.1.call-start = ((), (), s32[]{:S(2)}) async-start(), calls=%async_computation.6 | async-start | bytes 1048576 | tf_op jit(solution)/shard_map/psum | solution.py:72
  393.8 3.4 copy-start.1
  399.0 5.1 copy-start.4
  405.3 95.8 %all-gather.8.cloned.1.call-start = ((), (), s32[]{:S(2)}) async-start(), calls=%async_computation.7 | async-start | bytes 4325376 | tf_op jit(solution)/shard_map/all_gather | solution.py:43
  454.1 159.5 %all-reduce.15.cloned.1.call-start = ((), (), s32[]{:S(2)}) async-start(), calls=%async_computation.8 | async-start | bytes 8388608 | tf_op jit(solution)/shard_map/psum | solution.py:57
  521.4 146.7 %all-reduce.17.cloned.1.call-start = ((), (), s32[]{:S(2)}) async-start(), calls=%async_computation.9 | async-start | bytes 1048576 | tf_op jit(solution)/shard_map/psum | solution.py:72
  613.6 3.4 copy-start.2
Sparse Core Ops, SparseCore 0:
  10.8 48.6 all-gather.3
  80.1 92.1 all-reduce.6
  184.7 42.9 all-reduce.8
  233.5 46.7 all-gather.5
  301.7 92.0 all-reduce.10
  405.4 42.9 all-reduce.12
  454.2 46.7 all-gather.7
  521.5 92.0 all-reduce.14
  625.1 42.9 all-reduce.16
where the time goes:
time: 680 us; the launch traced here: 679 us
  waiting for transfers between devices  457 us (67%)
  local copies, waits for them, and re-layouts  104 us (15%)
  matrix products  53.1 us (8%)
  other arithmetic  42.1 us (6%)
  between operations  14.2 us (2%)
  starting transfers between devices  9.06 us (1%)
    psum x3, waiting for transfers between devices, body(): lax.psum(edge_term.astype(jnp.bfloat16), 'feat').astype(jnp.float32)  272 us
    psum x3, waiting for transfers between devices, body(): lax.psum(node_term.astype(jnp.bfloat16), 'feat').astype(jnp.float32)  123 us
    all_gather x3, waiting for transfers between devices, body(): every_proj = lax.all_gather(sender_proj, 'patch', axis=0, tiled=True)  61.4 us
    gather x3, local copies, waits for them, and re-layouts, body(): fetched = every_proj[senders]  41.3 us
    gather x3, local copies, waits for them, and re-layouts, body(): receiver_proj[receivers].astype(jnp.float32)  36.4 us
    gather x1, local copies, waits for them, and re-layouts, body(): remote_rows.reshape(-1)[edge_slot]  23 us
    dot_general x3, matrix products, body(): jnp.dot(edge_hidden, edge_out_w[layer_idx], preferred_element_type=jnp.fl...  20.7 us
    dot_general x3, matrix products, body(): jnp.dot(incoming, node_in_w[layer_idx, 1], preferred_element_type=jnp.flo...  15.3 us
  transfers between devices with their start and end apart: 10, of which 9 were waited for; matrix products, arithmetic and copies ran while one was open for 12% of the time, Pallas kernels for 0%

commit v1 on v0

v1 whole, which is shorter than its diff:
```python
import functools

import jax
import jax.numpy as jnp
from jax import lax
from jax.experimental import pallas as pl
from jax.experimental.pallas import tpu as pltpu
from jax.sharding import PartitionSpec as P

LAYERS = 3
CHUNKS = 2
BLOCK = 512
BF16 = jnp.bfloat16
F32 = jnp.float32
BIAS_ROWS = 16


def mm(a, b):
    return jnp.dot(a, b, preferred_element_type=F32)


def silu(v):
    half = 0.5 * v
    return half + half * jnp.tanh(half)


def norm(values, gain):
    center = values - jnp.mean(values, axis=-1, keepdims=True)
    spread = jnp.mean(center * center, axis=-1, keepdims=True)
    return center * lax.rsqrt(spread + 1e-05) * gain


def params():
    return pltpu.CompilerParams(vmem_limit_bytes=58 * 1024 * 1024)


def bundle_kernel(layer, ein_ref, eout_ref, nin_ref, nout_ref, nb_ref, out_ref):
    d, w = ein_ref.shape
    parts = d // w
    out_ref[0:d] = ein_ref[...]
    for j in range(parts):
        out_ref[d + j * w : d + (j + 1) * w] = eout_ref[:, j * w : (j + 1) * w]
        out_ref[4 * d + j * w : 4 * d + (j + 1) * w] = nout_ref[:, j * w : (j + 1) * w]
    out_ref[2 * d : 3 * d] = nin_ref[0]
    out_ref[3 * d : 4 * d] = nin_ref[1]
    bias = nb_ref[layer : layer + 1, :]
    first = bias.astype(BF16).astype(F32)
    second = (bias - first).astype(BF16).astype(F32)
    third = bias - first - second
    row = lax.broadcasted_iota(jnp.int32, (BIAS_ROWS, w), 0)
    terms = jnp.where(row == 0, first, jnp.where(row == 1, second, jnp.where(row == 2, third, 0.0)))
    out_ref[5 * d : 5 * d + BIAS_ROWS] = terms.astype(BF16)


def bundle(layer, edge_in_w, edge_out_w, node_in_w, node_out_w, node_in_b):
    d, w = edge_in_w.shape[2:]
    rows = 5 * d + BIAS_ROWS
    return pl.pallas_call(
        functools.partial(bundle_kernel, layer),
        grid=(1,),
        out_shape=jax.ShapeDtypeStruct((rows, w), BF16),
        in_specs=[
            pl.BlockSpec((None, None, d, w), lambda i: (layer, 0, 0, 0)),
            pl.BlockSpec((None, w, d), lambda i: (layer, 0, 0)),
            pl.BlockSpec((None, 2, d, w), lambda i: (layer, 0, 0, 0)),
            pl.BlockSpec((None, w, d), lambda i: (layer, 0, 0)),
            pl.BlockSpec(node_in_b.shape, lambda i: (0, 0)),
        ],
        out_specs=pl.BlockSpec((rows, w), lambda i: (0, 0)),
        compiler_params=params(),
        name="bundle",
    )(edge_in_w, edge_out_w, node_in_w, node_out_w, node_in_b)


def project(layer, state, ws_ref, wr_ref, eb_ref, rows_ref, slots_ref, recv_ref):
    sender = mm(state, ws_ref[...]).astype(BF16)
    recv_ref[...] = mm(state, wr_ref[...]) + eb_ref[layer : layer + 1, :]
    n = state.shape[0]
    peers, width = rows_ref.shape
    lanes = lax.broadcasted_iota(jnp.int32, (width, width), 1)

    def one(p, carry):
        index = jnp.broadcast_to(rows_ref[pl.ds(p, 1), :], (width, width)).T
        hot = jnp.concatenate(
            [jnp.where(index == lanes + j * width, 1.0, 0.0).astype(BF16) for j in range(n // width)], axis=1
        )
        slots_ref[pl.ds(p, 1)] = mm(hot, sender).astype(BF16)[None]
        return carry

    lax.fori_loop(0, peers, one, 0, unroll=4)


def first_kernel(node_ref, ws_ref, wr_ref, eb_ref, rows_ref, slots_ref, recv_ref):
    project(0, node_ref[...], ws_ref, wr_ref, eb_ref, rows_ref, slots_ref, recv_ref)


def project_specs(layer, edge_in_w, edge_in_b, send_rows):
    d, w = edge_in_w.shape[2:]
    return [
        pl.BlockSpec((None, None, d, w), lambda i: (layer, 1, 0, 0)),
        pl.BlockSpec((None, None, d, w), lambda i: (layer, 2, 0, 0)),
        pl.BlockSpec(edge_in_b.shape, lambda i: (0, 0)),
        pl.BlockSpec((None,) + send_rows.shape[1:], lambda i: (0, 0, 0)),
    ]


def project_outs(n, w, send_rows):
    peers, width = send_rows.shape[1:]
    shapes = [jax.ShapeDtypeStruct((peers, width, w), BF16), jax.ShapeDtypeStruct((n, w), F32)]
    specs = [pl.BlockSpec((peers, width, w), lambda i: (0, 0, 0)), pl.BlockSpec((n, w), lambda i: (0, 0))]
    return shapes, specs


def first(node_state, edge_in_w, edge_in_b, send_rows):
    n = node_state.shape[0]
    shapes, specs = project_outs(n, edge_in_w.shape[3], send_rows)
    return pl.pallas_call(
        first_kernel,
        grid=(1,),
        out_shape=shapes,
        in_specs=[pl.BlockSpec(node_state.shape, lambda i: (0, 0))]
        + project_specs(0, edge_in_w, edge_in_b, send_rows),
        out_specs=specs,
        compiler_params=params(),
        name="first",
    )(node_state, edge_in_w, edge_in_w, edge_in_b, send_rows)


def pick_kernel(start, slot_ref, recv_ref, table_ref, proj_ref, out_ref, wide_ref, acc_ref):
    wide_ref[...] = table_ref[...].astype(F32)
    group = 16

    def some(i, carry):
        base = i * group
        for r in range(group):
            s = slot_ref[start + base + r]
            q = recv_ref[start + base + r]
            acc_ref[pl.ds(base + r, 1), :] = wide_ref[pl.ds(s, 1), :] + proj_ref[pl.ds(q, 1), :]
        return carry

    lax.fori_loop(0, out_ref.shape[0] // group, some, 0)
    out_ref[...] = acc_ref[...].astype(BF16)


def pick(chunk, count, edge_slot, receivers, table, proj):
    w = table.shape[1]
    return pl.pallas_call(
        functools.partial(pick_kernel, chunk * count),
        grid=(1,),
        out_shape=jax.ShapeDtypeStruct((count, w), BF16),
        in_specs=[
            pl.BlockSpec(memory_space=pltpu.SMEM),
            pl.BlockSpec(memory_space=pltpu.SMEM),
            pl.BlockSpec(table.shape, lambda i: (0, 0)),
            pl.BlockSpec(proj.shape, lambda i: (0, 0)),
        ],
        out_specs=pl.BlockSpec((count, w), lambda i: (0, 0)),
        scratch_shapes=[pltpu.VMEM(table.shape, F32), pltpu.VMEM((count, w), F32)],
        compiler_params=params(),
        name="pick",
    )(edge_slot, receivers, table, proj)


def edge_kernel(layer, chunk, blocks, more, *refs):
    refs = list(refs)

    def take(k):
        got = refs[:k]
        del refs[:k]
        return got

    (x_ref,) = take(1)
    pre_refs = take(4)
    weight_refs = take(4)
    recv_ref, gain_ref = take(2)
    last_chunk = chunk == CHUNKS - 1
    if chunk > 0:
        _, before_ref = take(2)
    if last_chunk:
        node_ref, ngain_ref = take(2)
        nw_refs = [take(4) for _ in range(4)]
        if more:
            proj_in = take(4)
    (edge_out_ref,) = take(1)
    if last_chunk:
        (node_out_ref,) = take(1)
        if more:
            proj_out = take(2)
    else:
        (sum_ref,) = take(1)
    w0_ref, w1_ref = take(2)
    if last_chunk:
        (sum_ref,) = take(1)

    step = pl.program_id(0)
    w = pre_refs[0].shape[1]
    d = x_ref.shape[1]

    @pl.when(step == 0)
    def _():
        for j, ref in enumerate(weight_refs):
            w0_ref[:, j * w : (j + 1) * w] = ref[0:d]
            for k in range(d // w):
                w1_ref[j * w : (j + 1) * w, k * w : (k + 1) * w] = ref[d + k * w : d + (k + 1) * w]
        if chunk > 0:
            sum_ref[...] = before_ref[...]
        else:
            sum_ref[...] = jnp.zeros_like(sum_ref)

    x = x_ref[...]
    extra = jnp.concatenate([ref[...] for ref in pre_refs], axis=1).astype(F32)
    hidden = silu(mm(x, w0_ref[...]) + extra).astype(BF16)
    message = norm(mm(hidden, w1_ref[...]), gain_ref[layer : layer + 1, :])
    edge_out_ref[...] = (x.astype(F32) + message).astype(BF16)
    n = sum_ref.shape[0]
    ids = lax.broadcasted_iota(jnp.int32, (n, x.shape[0]), 0)
    hot = jnp.where(ids == recv_ref[...], 1.0, 0.0).astype(BF16)
    sum_ref[...] += mm(hot, message.astype(BF16))

    if last_chunk:

        @pl.when(step == blocks - 1)
        def _():
            node = node_ref[...]
            incoming = sum_ref[...].astype(BF16)
            for j in range(4):
                w0_ref[:, j * w : (j + 1) * w] = nw_refs[0][j][...]
                w1_ref[:, j * w : (j + 1) * w] = nw_refs[1][j][...]
            bias = jnp.concatenate(
                [jnp.sum(nw_refs[3][j][...].astype(F32), axis=0, keepdims=True) for j in range(4)], axis=1
            )
            node_hidden = silu(mm(node, w0_ref[...]) + mm(incoming, w1_ref[...]) + bias).astype(BF16)
            for j in range(4):
                for k in range(d // w):
                    w0_ref[j * w : (j + 1) * w, k * w : (k + 1) * w] = nw_refs[2][j][k * w : (k + 1) * w]
            change = norm(mm(node_hidden, w0_ref[...]), ngain_ref[layer : layer + 1, :])
            state = (node.astype(F32) + change).astype(BF16)
            node_out_ref[...] = state
            if more:
                project(layer + 1, state, *proj_in, *proj_out)


def edges(layer, chunk, edge_state, pres, bundles, receivers, edge_gain, carried, node_args, proj_args):
    total, d = edge_state.shape
    count = total // CHUNKS
    blocks = count // BLOCK
    base = chunk * blocks
    w = pres[0].shape[1]
    last_chunk = chunk == CHUNKS - 1
    more = proj_args is not None
    whole = lambda a: pl.BlockSpec(a.shape, lambda i: (0,) * a.ndim)
    args = [edge_state, *pres, *bundles, receivers, edge_gain]
    specs = [pl.BlockSpec((BLOCK, d), lambda i: (base + i, 0))]
    specs += [pl.BlockSpec((BLOCK, w), lambda i: (i, 0))] * 4
    specs += [pl.BlockSpec((2 * d, w), lambda i: (0, 0))] * 4
    specs += [pl.BlockSpec((1, BLOCK), lambda i: (0, base + i)), whole(edge_gain)]
    aliases = {}
    if chunk > 0:
        aliases = {len(args): 0}
        args += list(carried)
        specs += [pl.BlockSpec(memory_space=pl.ANY), whole(carried[1])]
    shapes = [jax.ShapeDtypeStruct((total, d), BF16)]
    outs = [pl.BlockSpec((BLOCK, d), lambda i: (base + i, 0))]
    n = node_args[0].shape[0]
    scratch = [pltpu.VMEM((d, d), BF16), pltpu.VMEM((d, d), BF16)]
    if last_chunk:
        node_state, node_gain = node_args
        args += [node_state, node_gain]
        specs += [whole(node_state), whole(node_gain)]
        for part in range(2, 5):
            args += list(bundles)
            specs += [pl.BlockSpec((d, w), lambda i, part=part: (part, 0))] * 4
        args += list(bundles)
        specs += [pl.BlockSpec((BIAS_ROWS, w), lambda i: (5 * d // BIAS_ROWS, 0))] * 4
        shapes.append(jax.ShapeDtypeStruct((n, d), BF16))
        outs.append(pl.BlockSpec((n, d), lambda i: (0, 0)))
        if more:
            edge_in_w, edge_in_b, send_rows = proj_args
            args += [edge_in_w, edge_in_w, edge_in_b, send_rows]
            specs += project_specs(layer + 1, edge_in_w, edge_in_b, send_rows)
            more_shapes, more_specs = project_outs(n, w, send_rows)
            shapes += more_shapes
            outs += more_specs
        scratch.append(pltpu.VMEM((n, d), F32))
    else:
        shapes.append(jax.ShapeDtypeStruct((n, d), F32))
        outs.append(pl.BlockSpec((n, d), lambda i: (0, 0)))
    return pl.pallas_call(
        functools.partial(edge_kernel, layer, chunk, blocks, more),
        grid=(blocks,),
        out_shape=shapes,
        in_specs=specs,
        out_specs=outs,
        scratch_shapes=scratch,
        input_output_aliases=aliases,
        compiler_params=params(),
        name="edges",
    )(*args)


def body(
    node_latents,
    edge_latents,
    send_rows,
    edge_slot,
    receivers,
    edge_in_w,
    edge_in_b,
    edge_out_w,
    edge_gain,
    node_in_w,
    node_in_b,
    node_out_w,
    node_gain,
):
    feat = lax.axis_size("feat")
    count = edge_latents.shape[0] // CHUNKS
    receiver_row = receivers.reshape(1, -1)

    def shift(value, by):
        return lax.ppermute(value, "feat", [(i, (i + by) % feat) for i in range(feat)])

    def gathered(layer):
        own = bundle(layer, edge_in_w, edge_out_w, node_in_w, node_out_w, node_in_b)
        return own

    edge_state = edge_latents
    node_state = node_latents
    slots, recv_proj = first(node_state, edge_in_w, edge_in_b, send_rows)
    for layer in range(LAYERS):
        own = bundle(layer, edge_in_w, edge_out_w, node_in_w, node_out_w, node_in_b)
        slots, own = lax.optimization_barrier((slots, own))
        bundles = (own, shift(own, 1), shift(own, -1), shift(own, 2))
        table = lax.all_to_all(slots, "patch", split_axis=0, concat_axis=0, tiled=True)
        table = table.reshape(-1, table.shape[2])
        near = []
        for chunk in range(CHUNKS):
            mine = pick(chunk, count, edge_slot, receivers, table, recv_proj)
            left, right = shift(mine, 1), shift(mine, -1)
            far = shift(left, 1) if chunk % 2 == 0 else shift(right, -1)
            near.append((mine, left, right, far))
        carried = None
        for chunk in range(CHUNKS):
            last = chunk == CHUNKS - 1
            proj_args = (edge_in_w, edge_in_b, send_rows) if last and layer < LAYERS - 1 else None
            carried = edges(
                layer, chunk, edge_state, near[chunk], bundles, receiver_row, edge_gain, carried,
                (node_state, node_gain), proj_args,
            )
        if layer < LAYERS - 1:
            edge_state, node_state, slots, recv_proj = carried
        else:
            edge_state, node_state = carried
    return (node_state, edge_state)


def solution(mesh):
    in_specs = (
        P("patch", None),
        P("patch", None),
        P("patch", None, None),
        P("patch"),
        P("patch"),
        P(None, None, None, "feat"),
        P(None, "feat"),
        P(None, "feat", None),
        P(),
        P(None, None, None, "feat"),
        P(None, "feat"),
        P(None, "feat", None),
        P(),
    )
    out_specs = (P("patch", None), P("patch", None))
    return jax.shard_map(body, mesh=mesh, in_specs=in_specs, out_specs=out_specs, check_vma=False)
```

time: 680 us -> 313 us (0.46)
  waiting for transfers between devices: 457 us -> 114 us
  Pallas kernels: 0 us -> 113 us
  local copies, waits for them, and re-layouts: 104 us -> 7.53 us
  starting transfers between devices: 9.06 us -> 76.5 us
  matrix products: 53.1 us -> 0 us
  other arithmetic: 42.1 us -> 0 us
  between operations: 14.2 us -> 1.07 us
    psum x6 -> x0, waiting for transfers between devices: 395 us -> none  [the longest x3 272 us: body(): lax.psum(edge_term.astype(jnp.bfloat16), 'feat').astype(jnp.float32)]
    pallas_call x0 -> x16, Pallas kernels: none -> 113 us  [the longest x6 68.1 us: edges(): pl.pallas_call(functools.partial(edge_kernel, layer, chunk, blocks, more)...]
    gather x7 -> x0, local copies, waits for them, and re-layouts: 101 us -> none  [the longest x3 41.3 us: body(): fetched = every_proj[senders]]
    ppermute x0 -> x27, waiting for transfers between devices: none -> 71.8 us  [shift(): lax.ppermute(value, 'feat', [(i, (i + by) % feat) for i in range(feat)])]
    all_gather x3 -> x0, waiting for transfers between devices: 61.4 us -> none  [body(): every_proj = lax.all_gather(sender_proj, 'patch', axis=0, tiled=True)]
    ppermute x0 -> x27, starting transfers between devices: none -> 60.1 us  [shift(): lax.ppermute(value, 'feat', [(i, (i + by) % feat) for i in range(feat)])]
    dot_general x18 -> x0, matrix products: 53.1 us -> none  [the longest x3 20.7 us: body(): jnp.dot(edge_hidden, edge_out_w[layer_idx], preferred_element_type=jnp.fl...]
    all_to_all x1 -> x3, waiting for transfers between devices: 0.01 us -> 41.7 us  [body(): lax.all_to_all(slots, 'patch', split_axis=0, concat_axis=0, tiled=True)]
  transfers between devices with their start and end apart: 10 -> 30, of which waited for: 9 -> 15; matrix products, arithmetic and copies ran while one was open for 12% -> 0% of each run, Pallas kernels for 0% -> 21%
where the time goes in v1:
time: 313 us; the launch traced here: 312 us
  waiting for transfers between devices  114 us (36%)
  Pallas kernels  113 us (36%)
  starting transfers between devices  76.5 us (24%)
  local copies, waits for them, and re-layouts  7.53 us (2%)
    ppermute x27, waiting for transfers between devices, shift(): lax.ppermute(value, 'feat', [(i, (i + by) % feat) for i in range(feat)])  71.8 us
    pallas_call x6, Pallas kernels, edges(): pl.pallas_call(functools.partial(edge_kernel, layer, chunk, blocks, more)...  68.1 us
    ppermute x27, starting transfers between devices, shift(): lax.ppermute(value, 'feat', [(i, (i + by) % feat) for i in range(feat)])  60.1 us
    all_to_all x3, waiting for transfers between devices, body(): lax.all_to_all(slots, 'patch', split_axis=0, concat_axis=0, tiled=True)  41.7 us
    pallas_call x6, Pallas kernels, pick(): pl.pallas_call(functools.partial(pick_kernel, chunk * count), grid=(1,),...  33.6 us
    all_to_all x3, starting transfers between devices, body(): lax.all_to_all(slots, 'patch', split_axis=0, concat_axis=0, tiled=True)  16.4 us
    unnamed x64, local copies, waits for them, and re-layouts  7.53 us
  transfers between devices with their start and end apart: 30, of which 15 were waited for; matrix products, arithmetic and copies ran while one was open for 0% of the time, Pallas kernels for 21%

profile of v1, /device:TPU:0, one launch (start us, length us, event | category | flops | bytes accessed | tf_op | source)
XLA Modules:
  0.0 311.9 jit_solution(17339902233610733032)
XLA Ops:
  0.6 5.3 %first.1 = (bf16[32,128,128]{2,1,0:T(8,128)(2,1)}, f32[512,128]{1,0:T(8,128)}) custom-call(bf16[512,512]{1,0:T(8,128)(2,1)} %refs_13_.1, bf16[3,3,512,128]{3,2,1,0:T(8,128)(2,1)} %ein_ref.5, bf16[3,3,512,128]{3,2,1,0:T(8,128)(2,1)} %ein_ref.5, f32[3,128]{1,0:T(4,128)} %refs_33_.3, s32[1,32,128]{2,1,0:T(8,128)} %refs_34_.3), custom_call_target="tpu_custom_call" | custom-call | tf_op jit(solution)/shard_map/first/pallas_call | solution.py:117
  6.0 2.1 bundle.3.refs_5_.refs_15_.refs_19_.refs_23_.refs_27_
  8.0 8.5 %all-to-all-start = ((bf16[32,128,128]{2,1,0:T(8,128)(2,1)}), bf16[32,128,128]{2,1,0:T(8,128)(2,1)}, u32[]{:S(2)}, u32[]{:S(2)}) async-start(bf16[32,128,128]{2,1,0:T(8,128)(2,1)} %get-tuple-element.27), calls=%async_computation | async-start | bytes 2097152 | tf_op jit(solution)/shard_map/all_to_all | solution.py:334
  16.6 1.6 collective-permute-start.3
  18.2 1.7 collective-permute-start.4
  19.9 13.9 %all-to-all-done = bf16[32,128,128]{2,1,0:T(8,128)(2,1)} async-done(((bf16[32,128,128]{2,1,0:T(8,128)(2,1)}), bf16[32,128,128]{2,1,0:T(8,128)(2,1)}, u32[]{:S(2)}, u32[]{:S(2)}) %all-to-all-start) | async-done | bytes 1048608 | tf_op jit(solution)/shard_map/all_to_all | solution.py:334
  33.8 5.6 %pick.7.refs_1_ = bf16[2048,128]{1,0:T(8,128)(2,1)} custom-call(s32[4096]{0:T(1024)} %slot_ref.11, s32[4096]{0:T(1024)} %recv_ref.11, bf16[4096,128]{1,0:T(8,128)(2,1)} %bitcast.table_ref, f32[512,128]{1,0:T(8,128)} %get-tuple-element.28.proj_ref), custom_call_target="tpu_custom_call" | custom-call | tf_op jit(solution)/shard_map/pick/pallas_call | solution.py:147
  39.3 1.6 collective-permute-start.6
  40.9 5.6 %pick.6.refs_1_ = bf16[2048,128]{1,0:T(8,128)(2,1)} custom-call(s32[4096]{0:T(1024)} %slot_ref.11, s32[4096]{0:T(1024)} %recv_ref.11, bf16[4096,128]{1,0:T(8,128)(2,1)} %bitcast.table_ref, f32[512,128]{1,0:T(8,128)} %get-tuple-element.28.proj_ref), custom_call_target="tpu_custom_call" | custom-call | tf_op jit(solution)/shard_map/pick/pallas_call | solution.py:147
  46.5 1.7 collective-permute-start.1
  48.2 2.0 collective-permute-start.5
  50.2 1.1 collective-permute-start.7
  51.2 3.5 %collective-permute-done.6.refs_2_ = bf16[2048,128]{1,0:T(8,128)(2,1)S(1)} collective-permute-done((bf16[2048,128]{1,0:T(8,128)(2,1)}, bf16[2048,128]{1,0:T(8,128)(2,1)S(1)}, u32[]{:S(2)}, u32[]{:S(2)}) %collective-permute-start.6) | collective-permute-done | bytes 524320 | tf_op jit(solution)/shard_map/ppermute | solution.py:321
  54.8 1.2 collective-permute-start.8
  55.9 14.1 %collective-permute-start = (bf16[2048,128]{1,0:T(8,128)(2,1)}, bf16[2048,128]{1,0:T(8,128)(2,1)S(1)}, u32[]{:S(2)}, u32[]{:S(2)}) collective-permute-start(bf16[2048,128]{1,0:T(8,128)(2,1)} %pick.6.refs_1_), channel_id=1, source_target_pairs={{0,1},{1,2},{2,3},{3,0},{4,5},{5,6},{6,7},{7,4},{8,9},{9,10},{10,1... | collective-permute-start | bytes 1572872 | tf_op jit(solution)/shard_map/ppermute | solution.py:321
  70.0 4.6 %collective-permute-done.1.refs_3_ = bf16[2048,128]{1,0:T(8,128)(2,1)S(1)} collective-permute-done((bf16[2048,128]{1,0:T(8,128)(2,1)}, bf16[2048,128]{1,0:T(8,128)(2,1)S(1)}, u32[]{:S(2)}, u32[]{:S(2)}) %collective-permute-start.1) | collective-permute-done | bytes 524320 | tf_op jit(solution)/shard_map/ppermute | solution.py:321
  74.6 3.9 %collective-permute-start.2 = (bf16[2048,128]{1,0:T(8,128)(2,1)S(1)}, bf16[2048,128]{1,0:T(8,128)(2,1)S(1)}, u32[]{:S(2)}, u32[]{:S(2)}) collective-permute-start(bf16[2048,128]{1,0:T(8,128)(2,1)S(1)} %collective-permute-done.1.refs_3_), channel_id=1, source_target_pairs={{0,3},{1,0},{2,1},{3,2},{4,7},{5,4},{6,5},{7,6},{8,11},{9,8},{10,9... | collective-permute-start | bytes 1572872 | tf_op jit(solution)/shard_map/ppermute | solution.py:321
  78.6 2.1 bundle.4.refs_5_.refs_15_.refs_19_.refs_23_.refs_27_
  80.6 6.3 %collective-permute-done.7.refs_3_ = bf16[2048,128]{1,0:T(8,128)(2,1)S(1)} collective-permute-done((bf16[2048,128]{1,0:T(8,128)(2,1)}, bf16[2048,128]{1,0:T(8,128)(2,1)S(1)}, u32[]{:S(2)}, u32[]{:S(2)}) %collective-permute-start.7) | collective-permute-done | bytes 524320 | tf_op jit(solution)/shard_map/ppermute | solution.py:321
  87.0 0.8 copy-done.24
  88.0 8.9 %edges.6 = (bf16[4096,512]{1,0:T(8,128)(2,1)}, f32[512,512]{1,0:T(8,128)}) custom-call(bf16[4096,512]{1,0:T(8,128)(2,1)} %refs_0_.3, bf16[2048,128]{1,0:T(8,128)(2,1)} %pick.7.refs_1_, bf16[2048,128]{1,0:T(8,128)(2,1)} %copy-done.17, bf16[2048,128]{1,0:T(8,128)(2,1)} %copy-done.24, bf16[2048,128]{1,0:T(8,128)(2,1)} %copy-done.29, ...), custom_call_target="tpu_custom_call" | custom-call | tf_op jit(solution)/shard_map/edges/pallas_call | solution.py:288
  97.1 0.7 copy-done.21
  98.0 15.0 %edges.7 = (bf16[4096,512]{1,0:T(8,128)(2,1)}, bf16[512,512]{1,0:T(8,128)(2,1)}, bf16[32,128,128]{2,1,0:T(8,128)(2,1)}, f32[512,128]{1,0:T(8,128)}) custom-call(bf16[4096,512]{1,0:T(8,128)(2,1)} %refs_0_.3, bf16[2048,128]{1,0:T(8,128)(2,1)} %pick.6.refs_1_, bf16[2048,128]{1,0:T(8,128)(2,1)} %copy-done.21, ...), custom_call_target="tpu_custom_call", output_to_operand_aliasing={{0}: (11, {})} | custom-call | tf_op jit(solution)/shard_map/edges/pallas_call | solution.py:288
  113.0 3.9 %all-to-all-start.1 = ((bf16[32,128,128]{2,1,0:T(8,128)(2,1)}), bf16[32,128,128]{2,1,0:T(8,128)(2,1)S(1)}, u32[]{:S(2)}, u32[]{:S(2)}) async-start(bf16[32,128,128]{2,1,0:T(8,128)(2,1)} %get-tuple-element.34), calls=%async_computation.1 | async-start | bytes 2097152 | tf_op jit(solution)/shard_map/all_to_all | solution.py:334
  116.9 1.6 collective-permute-start.12
  118.6 1.7 collective-permute-start.13
  120.2 13.9 %all-to-all-done.1 = bf16[32,128,128]{2,1,0:T(8,128)(2,1)S(1)} async-done(((bf16[32,128,128]{2,1,0:T(8,128)(2,1)}), bf16[32,128,128]{2,1,0:T(8,128)(2,1)S(1)}, u32[]{:S(2)}, u32[]{:S(2)}) %all-to-all-start.1) | async-done | bytes 1048608 | tf_op jit(solution)/shard_map/all_to_all | solution.py:334
  134.1 1.0 copy-done.12
  135.2 5.6 %pick.9.refs_1_ = bf16[2048,128]{1,0:T(8,128)(2,1)} custom-call(s32[4096]{0:T(1024)} %slot_ref.11, s32[4096]{0:T(1024)} %recv_ref.11, bf16[4096,128]{1,0:T(8,128)(2,1)} %bitcast.4, f32[512,128]{1,0:T(8,128)} %get-tuple-element.35.proj_ref), custom_call_target="tpu_custom_call" | custom-call | tf_op jit(solution)/shard_map/pick/pallas_call | solution.py:147
  140.7 1.6 collective-permute-start.15
  142.3 5.6 %pick.8.refs_1_ = bf16[2048,128]{1,0:T(8,128)(2,1)} custom-call(s32[4096]{0:T(1024)} %slot_ref.11, s32[4096]{0:T(1024)} %recv_ref.11, bf16[4096,128]{1,0:T(8,128)(2,1)} %bitcast.5, f32[512,128]{1,0:T(8,128)} %get-tuple-element.35.proj_ref), custom_call_target="tpu_custom_call" | custom-call | tf_op jit(solution)/shard_map/pick/pallas_call | solution.py:147
  147.9 1.7 collective-permute-start.10
  149.6 1.7 collective-permute-start.14
  151.3 1.3 collective-permute-start.16
  152.6 3.5 %collective-permute-done.15.refs_2_ = bf16[2048,128]{1,0:T(8,128)(2,1)S(1)} collective-permute-done((bf16[2048,128]{1,0:T(8,128)(2,1)}, bf16[2048,128]{1,0:T(8,128)(2,1)S(1)}, u32[]{:S(2)}, u32[]{:S(2)}) %collective-permute-start.15) | collective-permute-done | bytes 524320 | tf_op jit(solution)/shard_map/ppermute | solution.py:321
  156.1 1.2 collective-permute-start.17
  157.3 1.2 collective-permute-start.9
  158.5 17.5 %collective-permute-done.10.refs_3_ = bf16[2048,128]{1,0:T(8,128)(2,1)S(1)} collective-permute-done((bf16[2048,128]{1,0:T(8,128)(2,1)}, bf16[2048,128]{1,0:T(8,128)(2,1)S(1)}, u32[]{:S(2)}, u32[]{:S(2)}) %collective-permute-start.10) | collective-permute-done | bytes 524320 | tf_op jit(solution)/shard_map/ppermute | solution.py:321
  176.0 3.9 %collective-permute-start.11 = (bf16[2048,128]{1,0:T(8,128)(2,1)S(1)}, bf16[2048,128]{1,0:T(8,128)(2,1)S(1)}, u32[]{:S(2)}, u32[]{:S(2)}) collective-permute-start(bf16[2048,128]{1,0:T(8,128)(2,1)S(1)} %collective-permute-done.10.refs_3_), channel_id=1, source_target_pairs={{0,3},{1,0},{2,1},{3,2},{4,7},{5,4},{6,5},{7,6},{8,11},{9,8},{10,9... | collective-permute-start | bytes 1572872 | tf_op jit(solution)/shard_map/ppermute | solution.py:321
  179.9 2.1 bundle.5.refs_5_.refs_15_.refs_19_.refs_23_.refs_27_
  182.1 6.3 %collective-permute-done.16.refs_3_ = bf16[2048,128]{1,0:T(8,128)(2,1)S(1)} collective-permute-done((bf16[2048,128]{1,0:T(8,128)(2,1)}, bf16[2048,128]{1,0:T(8,128)(2,1)S(1)}, u32[]{:S(2)}, u32[]{:S(2)}) %collective-permute-start.16) | collective-permute-done | bytes 524320 | tf_op jit(solution)/shard_map/ppermute | solution.py:321
  188.4 0.8 copy-done.26
  189.3 8.9 %edges.8 = (bf16[4096,512]{1,0:T(8,128)(2,1)}, f32[512,512]{1,0:T(8,128)}) custom-call(bf16[4096,512]{1,0:T(8,128)(2,1)} %get-tuple-element.32.refs_0_, bf16[2048,128]{1,0:T(8,128)(2,1)} %pick.9.refs_1_, bf16[2048,128]{1,0:T(8,128)(2,1)} %copy-done.18, bf16[2048,128]{1,0:T(8,128)(2,1)} %copy-done.26, bf16[2048,128]{1,0:T(8,128)(2,1)} %copy-done.30, ...), custom_call_target="tpu_custom_call" | custom-call | tf_op jit(solution)/shard_map/edges/pallas_call | solution.py:288
  199.3 15.1 %edges.9 = (bf16[4096,512]{1,0:T(8,128)(2,1)}, bf16[512,512]{1,0:T(8,128)(2,1)}, bf16[32,128,128]{2,1,0:T(8,128)(2,1)}, f32[512,128]{1,0:T(8,128)}) custom-call(bf16[4096,512]{1,0:T(8,128)(2,1)} %get-tuple-element.32.refs_0_, bf16[2048,128]{1,0:T(8,128)(2,1)} %pick.8.refs_1_, bf16[2048,128]{1,0:T(8,128)(2,1)} %copy-done.20, ...), custom_call_target="tpu_custom_call", output_to_operand_aliasing={{0}: (11, {})} | custom-call | tf_op jit(solution)/shard_map/edges/pallas_call | solution.py:288
  214.3 3.9 %all-to-all-start.2 = ((bf16[32,128,128]{2,1,0:T(8,128)(2,1)}), bf16[32,128,128]{2,1,0:T(8,128)(2,1)S(1)}, u32[]{:S(2)}, u32[]{:S(2)}) async-start(bf16[32,128,128]{2,1,0:T(8,128)(2,1)} %get-tuple-element.42), calls=%async_computation.2 | async-start | bytes 2097152 | tf_op jit(solution)/shard_map/all_to_all | solution.py:334
  218.3 1.4 collective-permute-start.21
  219.7 2.0 collective-permute-start.22
  221.6 13.9 %all-to-all-done.2 = bf16[32,128,128]{2,1,0:T(8,128)(2,1)S(1)} async-done(((bf16[32,128,128]{2,1,0:T(8,128)(2,1)}), bf16[32,128,128]{2,1,0:T(8,128)(2,1)S(1)}, u32[]{:S(2)}, u32[]{:S(2)}) %all-to-all-start.2) | async-done | bytes 1048608 | tf_op jit(solution)/shard_map/all_to_all | solution.py:334
  235.5 1.0 copy-done.13
  236.5 5.6 %pick.11.refs_1_ = bf16[2048,128]{1,0:T(8,128)(2,1)} custom-call(s32[4096]{0:T(1024)} %slot_ref.11, s32[4096]{0:T(1024)} %recv_ref.11, bf16[4096,128]{1,0:T(8,128)(2,1)} %bitcast.6, f32[512,128]{1,0:T(8,128)} %get-tuple-element.43.proj_ref), custom_call_target="tpu_custom_call" | custom-call | tf_op jit(solution)/shard_map/pick/pallas_call | solution.py:147
  242.0 1.3 collective-permute-start.24
  243.3 5.6 %pick.10.refs_1_ = bf16[2048,128]{1,0:T(8,128)(2,1)} custom-call(s32[4096]{0:T(1024)} %slot_ref.11, s32[4096]{0:T(1024)} %recv_ref.11, bf16[4096,128]{1,0:T(8,128)(2,1)} %bitcast.7, f32[512,128]{1,0:T(8,128)} %get-tuple-element.43.proj_ref), custom_call_target="tpu_custom_call" | custom-call | tf_op jit(solution)/shard_map/pick/pallas_call | solution.py:147
  248.9 2.0 collective-permute-start.19
  250.9 1.6 collective-permute-start.23
  252.5 1.2 collective-permute-start.25
  253.6 3.7 %collective-permute-done.24.refs_2_ = bf16[2048,128]{1,0:T(8,128)(2,1)S(1)} collective-permute-done((bf16[2048,128]{1,0:T(8,128)(2,1)}, bf16[2048,128]{1,0:T(8,128)(2,1)S(1)}, u32[]{:S(2)}, u32[]{:S(2)}) %collective-permute-start.24) | collective-permute-done | bytes 524320 | tf_op jit(solution)/shard_map/ppermute | solution.py:321
  257.4 0.9 collective-permute-start.26
  258.3 1.5 collective-permute-start.18
  259.8 17.7 %collective-permute-done.19.refs_3_ = bf16[2048,128]{1,0:T(8,128)(2,1)S(1)} collective-permute-done((bf16[2048,128]{1,0:T(8,128)(2,1)}, bf16[2048,128]{1,0:T(8,128)(2,1)S(1)}, u32[]{:S(2)}, u32[]{:S(2)}) %collective-permute-start.19) | collective-permute-done | bytes 524320 | tf_op jit(solution)/shard_map/ppermute | solution.py:321
  277.5 3.7 %collective-permute-start.20 = (bf16[2048,128]{1,0:T(8,128)(2,1)S(1)}, bf16[2048,128]{1,0:T(8,128)(2,1)S(1)}, u32[]{:S(2)}, u32[]{:S(2)}) collective-permute-start(bf16[2048,128]{1,0:T(8,128)(2,1)S(1)} %collective-permute-done.19.refs_3_), channel_id=1, source_target_pairs={{0,3},{1,0},{2,1},{3,2},{4,7},{5,4},{6,5},{7,6},{8,11},{9,8},{10,9... | collective-permute-start | bytes 1572872 | tf_op jit(solution)/shard_map/ppermute | solution.py:321
  281.3 8.1 %collective-permute-done.25.refs_3_ = bf16[2048,128]{1,0:T(8,128)(2,1)S(1)} collective-permute-done((bf16[2048,128]{1,0:T(8,128)(2,1)}, bf16[2048,128]{1,0:T(8,128)(2,1)S(1)}, u32[]{:S(2)}, u32[]{:S(2)}) %collective-permute-start.25) | collective-permute-done | bytes 524320 | tf_op jit(solution)/shard_map/ppermute | solution.py:321
  289.4 0.7 copy-done.28
  290.4 8.9 %edges.10 = (bf16[4096,512]{1,0:T(8,128)(2,1)}, f32[512,512]{1,0:T(8,128)}) custom-call(bf16[4096,512]{1,0:T(8,128)(2,1)} %get-tuple-element.40.refs_0_, bf16[2048,128]{1,0:T(8,128)(2,1)} %pick.11.refs_1_, bf16[2048,128]{1,0:T(8,128)(2,1)} %copy-done.19, bf16[2048,128]{1,0:T(8,128)(2,1)} %copy-done.28, bf16[2048,128]{1,0:T(8,128)(2,1)} %copy-done.31, ...), custom_call_target="tpu_custom_call" | custom-call | tf_op jit(solution)/shard_map/edges/pallas_call | solution.py:288
  300.3 11.4 %edges.11 = (bf16[4096,512]{1,0:T(8,128)(2,1)}, bf16[512,512]{1,0:T(8,128)(2,1)}) custom-call(bf16[4096,512]{1,0:T(8,128)(2,1)} %get-tuple-element.40.refs_0_, bf16[2048,128]{1,0:T(8,128)(2,1)} %pick.10.refs_1_, bf16[2048,128]{1,0:T(8,128)(2,1)} %copy-done.22, bf16[2048,128]{1,0:T(8,128)(2,1)} %copy-done.16, ...), custom_call_target="tpu_custom_call", output_to_operand_aliasing={{0}: (11, {})} | custom-call | tf_op jit(solution)/shard_map/edges/pallas_call | solution.py:288
  (76 shorter events, 3.2 us)
Async XLA Ops:
  8.0 40.2 %copy-start.2 = (bf16[2576,128]{1,0:T(8,128)(2,1)S(1)}, bf16[2576,128]{1,0:T(8,128)(2,1)}, u32[]{:S(2)}) copy-start(bf16[2576,128]{1,0:T(8,128)(2,1)} %bundle.3.refs_5_.refs_15_.refs_19_.refs_23_.refs_27_) | copy-start | bytes 1978372
  8.0 25.7 %all-to-all-start = ((bf16[32,128,128]{2,1,0:T(8,128)(2,1)}), bf16[32,128,128]{2,1,0:T(8,128)(2,1)}, u32[]{:S(2)}, u32[]{:S(2)}) async-start(bf16[32,128,128]{2,1,0:T(8,128)(2,1)} %get-tuple-element.27), calls=%async_computation | async-start | bytes 2097152 | tf_op jit(solution)/shard_map/all_to_all | solution.py:334
  16.6 33.6 %collective-permute-start.3 = (bf16[2576,128]{1,0:T(8,128)(2,1)}, bf16[2576,128]{1,0:T(8,128)(2,1)S(1)}, u32[]{:S(2)}, u32[]{:S(2)}) collective-permute-start(bf16[2576,128]{1,0:T(8,128)(2,1)} %bundle.3.refs_5_.refs_15_.refs_19_.refs_23_.refs_27_), channel_id=1, source_target_pairs={{0,1},{1,2},{2,3},{3,0},{4,5},{5,6},{6,7},{7,4},{8,9},{9,10},{10,1... | collective-permute-start | bytes 1978376 | tf_op jit(solution)/shard_map/ppermute | solution.py:321
  18.2 37.7 %collective-permute-start.4 = (bf16[2576,128]{1,0:T(8,128)(2,1)}, bf16[2576,128]{1,0:T(8,128)(2,1)S(1)}, u32[]{:S(2)}, u32[]{:S(2)}) collective-permute-start(bf16[2576,128]{1,0:T(8,128)(2,1)} %bundle.3.refs_5_.refs_15_.refs_19_.refs_23_.refs_27_), channel_id=1, source_target_pairs={{0,3},{1,0},{2,1},{3,2},{4,7},{5,4},{6,5},{7,6},{8,11},{9,8},{10,9... | collective-permute-start | bytes 1978376 | tf_op jit(solution)/shard_map/ppermute | solution.py:321
  39.3 15.4 %collective-permute-start.6 = (bf16[2048,128]{1,0:T(8,128)(2,1)}, bf16[2048,128]{1,0:T(8,128)(2,1)S(1)}, u32[]{:S(2)}, u32[]{:S(2)}) collective-permute-start(bf16[2048,128]{1,0:T(8,128)(2,1)} %pick.7.refs_1_), channel_id=1, source_target_pairs={{0,1},{1,2},{2,3},{3,0},{4,5},{5,6},{6,7},{7,4},{8,9},{9,10},{10,1... | collective-permute-start | bytes 1572872 | tf_op jit(solution)/shard_map/ppermute | solution.py:321
  46.5 28.1 %collective-permute-start.1 = (bf16[2048,128]{1,0:T(8,128)(2,1)}, bf16[2048,128]{1,0:T(8,128)(2,1)S(1)}, u32[]{:S(2)}, u32[]{:S(2)}) collective-permute-start(bf16[2048,128]{1,0:T(8,128)(2,1)} %pick.6.refs_1_), channel_id=1, source_target_pairs={{0,3},{1,0},{2,1},{3,2},{4,7},{5,4},{6,5},{7,6},{8,11},{9,8},{10,9... | collective-permute-start | bytes 1572872 | tf_op jit(solution)/shard_map/ppermute | solution.py:321
  48.2 32.4 %collective-permute-start.5 = (bf16[2576,128]{1,0:T(8,128)(2,1)S(1)}, bf16[2576,128]{1,0:T(8,128)(2,1)S(1)}, u32[]{:S(2)}, u32[]{:S(2)}) collective-permute-start(bf16[2576,128]{1,0:T(8,128)(2,1)S(1)} %copy-done.2), channel_id=1, source_target_pairs={{0,2},{1,3},{2,0},{3,1},{4,6},{5,7},{6,4},{7,5},{8,10},{9,11},{10,... | collective-permute-start | bytes 1978376 | tf_op jit(solution)/shard_map/ppermute | solution.py:321
  50.2 36.8 %copy-start.4 = (bf16[2576,128]{1,0:T(8,128)(2,1)}, bf16[2576,128]{1,0:T(8,128)(2,1)S(1)}, u32[]{:S(2)}) copy-start(bf16[2576,128]{1,0:T(8,128)(2,1)S(1)} %collective-permute-done.3.refs_6_.refs_16_.refs_20_.refs_24_.refs_28_) | copy-start | bytes 1978372
  50.2 36.8 %collective-permute-start.7 = (bf16[2048,128]{1,0:T(8,128)(2,1)}, bf16[2048,128]{1,0:T(8,128)(2,1)S(1)}, u32[]{:S(2)}, u32[]{:S(2)}) collective-permute-start(bf16[2048,128]{1,0:T(8,128)(2,1)} %pick.7.refs_1_), channel_id=1, source_target_pairs={{0,3},{1,0},{2,1},{3,2},{4,7},{5,4},{6,5},{7,6},{8,11},{9,8},{10,9... | collective-permute-start | bytes 1572872 | tf_op jit(solution)/shard_map/ppermute | solution.py:321
  54.8 32.2 %copy-start.17 = (bf16[2048,128]{1,0:T(8,128)(2,1)}, bf16[2048,128]{1,0:T(8,128)(2,1)S(1)}, u32[]{:S(2)}) copy-start(bf16[2048,128]{1,0:T(8,128)(2,1)S(1)} %collective-permute-done.6.refs_2_) | copy-start | bytes 1572868
  54.8 32.2 %collective-permute-start.8 = (bf16[2048,128]{1,0:T(8,128)(2,1)S(1)}, bf16[2048,128]{1,0:T(8,128)(2,1)S(1)}, u32[]{:S(2)}, u32[]{:S(2)}) collective-permute-start(bf16[2048,128]{1,0:T(8,128)(2,1)S(1)} %collective-permute-done.6.refs_2_), channel_id=1, source_target_pairs={{0,1},{1,2},{2,3},{3,0},{4,5},{5,6},{6,7},{7,4},{8,9},{9,10},{10,1... | collective-permute-start | bytes 1572872 | tf_op jit(solution)/shard_map/ppermute | solution.py:321
  55.9 31.1 %copy-start.7 = (bf16[2576,128]{1,0:T(8,128)(2,1)}, bf16[2576,128]{1,0:T(8,128)(2,1)S(1)}, u32[]{:S(2)}) copy-start(bf16[2576,128]{1,0:T(8,128)(2,1)S(1)} %collective-permute-done.4.refs_7_.refs_17_.refs_21_.refs_25_.refs_29_) | copy-start | bytes 1978372
  55.9 41.0 %collective-permute-start = (bf16[2048,128]{1,0:T(8,128)(2,1)}, bf16[2048,128]{1,0:T(8,128)(2,1)S(1)}, u32[]{:S(2)}, u32[]{:S(2)}) collective-permute-start(bf16[2048,128]{1,0:T(8,128)(2,1)} %pick.6.refs_1_), channel_id=1, source_target_pairs={{0,1},{1,2},{2,3},{3,0},{4,5},{5,6},{6,7},{7,4},{8,9},{9,10},{10,1... | collective-permute-start | bytes 1572872 | tf_op jit(solution)/shard_map/ppermute | solution.py:321
  74.6 22.3 %copy-start.15 = (bf16[2048,128]{1,0:T(8,128)(2,1)}, bf16[2048,128]{1,0:T(8,128)(2,1)S(1)}, u32[]{:S(2)}) copy-start(bf16[2048,128]{1,0:T(8,128)(2,1)S(1)} %collective-permute-done.1.refs_3_) | copy-start | bytes 1572868
  74.6 22.4 %collective-permute-start.2 = (bf16[2048,128]{1,0:T(8,128)(2,1)S(1)}, bf16[2048,128]{1,0:T(8,128)(2,1)S(1)}, u32[]{:S(2)}, u32[]{:S(2)}) collective-permute-start(bf16[2048,128]{1,0:T(8,128)(2,1)S(1)} %collective-permute-done.1.refs_3_), channel_id=1, source_target_pairs={{0,3},{1,0},{2,1},{3,2},{4,7},{5,4},{6,5},{7,6},{8,11},{9,8},{10,9... | collective-permute-start | bytes 1572872 | tf_op jit(solution)/shard_map/ppermute | solution.py:321
  80.6 6.4 %copy-start.10 = (bf16[2576,128]{1,0:T(8,128)(2,1)}, bf16[2576,128]{1,0:T(8,128)(2,1)S(1)}, u32[]{:S(2)}) copy-start(bf16[2576,128]{1,0:T(8,128)(2,1)S(1)} %collective-permute-done.5.refs_8_.refs_18_.refs_22_.refs_26_.refs_30_) | copy-start | bytes 1978372
  87.0 0.8 copy-start.24
  87.0 1.1 copy-start.29
  96.9 0.8 copy-start.21
  97.1 0.9 copy-start.25
  98.0 19.0 %copy-start = (bf16[2576,128]{1,0:T(8,128)(2,1)S(1)}, bf16[2576,128]{1,0:T(8,128)(2,1)}, u32[]{:S(2)}) copy-start(bf16[2576,128]{1,0:T(8,128)(2,1)} %bundle.4.refs_5_.refs_15_.refs_19_.refs_23_.refs_27_) | copy-start | bytes 1978372
  113.0 21.2 %all-to-all-start.1 = ((bf16[32,128,128]{2,1,0:T(8,128)(2,1)}), bf16[32,128,128]{2,1,0:T(8,128)(2,1)S(1)}, u32[]{:S(2)}, u32[]{:S(2)}) async-start(bf16[32,128,128]{2,1,0:T(8,128)(2,1)} %get-tuple-element.34), calls=%async_computation.1 | async-start | bytes 2097152 | tf_op jit(solution)/shard_map/all_to_all | solution.py:334
  116.9 34.4 %collective-permute-start.12 = (bf16[2576,128]{1,0:T(8,128)(2,1)S(1)}, bf16[2576,128]{1,0:T(8,128)(2,1)S(1)}, u32[]{:S(2)}, u32[]{:S(2)}) collective-permute-start(bf16[2576,128]{1,0:T(8,128)(2,1)S(1)} %copy-done), channel_id=1, source_target_pairs={{0,1},{1,2},{2,3},{3,0},{4,5},{5,6},{6,7},{7,4},{8,9},{9,10},{10,1... | collective-permute-start | bytes 1978376 | tf_op jit(solution)/shard_map/ppermute | solution.py:321
  118.6 38.7 %collective-permute-start.13 = (bf16[2576,128]{1,0:T(8,128)(2,1)S(1)}, bf16[2576,128]{1,0:T(8,128)(2,1)S(1)}, u32[]{:S(2)}, u32[]{:S(2)}) collective-permute-start(bf16[2576,128]{1,0:T(8,128)(2,1)S(1)} %copy-done), channel_id=1, source_target_pairs={{0,3},{1,0},{2,1},{3,2},{4,7},{5,4},{6,5},{7,6},{8,11},{9,8},{10,9... | collective-permute-start | bytes 1978376 | tf_op jit(solution)/shard_map/ppermute | solution.py:321
  134.1 1.0 copy-start.12
  140.7 15.4 %collective-permute-start.15 = (bf16[2048,128]{1,0:T(8,128)(2,1)}, bf16[2048,128]{1,0:T(8,128)(2,1)S(1)}, u32[]{:S(2)}, u32[]{:S(2)}) collective-permute-start(bf16[2048,128]{1,0:T(8,128)(2,1)} %pick.9.refs_1_), channel_id=1, source_target_pairs={{0,1},{1,2},{2,3},{3,0},{4,5},{5,6},{6,7},{7,4},{8,9},{9,10},{10,1... | collective-permute-start | bytes 1572872 | tf_op jit(solution)/shard_map/ppermute | solution.py:321
  147.9 28.1 %collective-permute-start.10 = (bf16[2048,128]{1,0:T(8,128)(2,1)}, bf16[2048,128]{1,0:T(8,128)(2,1)S(1)}, u32[]{:S(2)}, u32[]{:S(2)}) collective-permute-start(bf16[2048,128]{1,0:T(8,128)(2,1)} %pick.8.refs_1_), channel_id=1, source_target_pairs={{0,3},{1,0},{2,1},{3,2},{4,7},{5,4},{6,5},{7,6},{8,11},{9,8},{10,9... | collective-permute-start | bytes 1572872 | tf_op jit(solution)/shard_map/ppermute | solution.py:321
  149.6 32.5 %collective-permute-start.14 = (bf16[2576,128]{1,0:T(8,128)(2,1)S(1)}, bf16[2576,128]{1,0:T(8,128)(2,1)S(1)}, u32[]{:S(2)}, u32[]{:S(2)}) collective-permute-start(bf16[2576,128]{1,0:T(8,128)(2,1)S(1)} %copy-done), channel_id=1, source_target_pairs={{0,2},{1,3},{2,0},{3,1},{4,6},{5,7},{6,4},{7,5},{8,10},{9,11},{10,... | collective-permute-start | bytes 1978376 | tf_op jit(solution)/shard_map/ppermute | solution.py:321
  151.3 37.0 %copy-start.3 = (bf16[2576,128]{1,0:T(8,128)(2,1)}, bf16[2576,128]{1,0:T(8,128)(2,1)S(1)}, u32[]{:S(2)}) copy-start(bf16[2576,128]{1,0:T(8,128)(2,1)S(1)} %collective-permute-done.12.refs_6_.refs_16_.refs_20_.refs_24_.refs_28_) | copy-start | bytes 1978372
  151.3 37.0 %collective-permute-start.16 = (bf16[2048,128]{1,0:T(8,128)(2,1)}, bf16[2048,128]{1,0:T(8,128)(2,1)S(1)}, u32[]{:S(2)}, u32[]{:S(2)}) collective-permute-start(bf16[2048,128]{1,0:T(8,128)(2,1)} %pick.9.refs_1_), channel_id=1, source_target_pairs={{0,3},{1,0},{2,1},{3,2},{4,7},{5,4},{6,5},{7,6},{8,11},{9,8},{10,9... | collective-permute-start | bytes 1572872 | tf_op jit(solution)/shard_map/ppermute | solution.py:321
  156.1 32.3 %copy-start.18 = (bf16[2048,128]{1,0:T(8,128)(2,1)}, bf16[2048,128]{1,0:T(8,128)(2,1)S(1)}, u32[]{:S(2)}) copy-start(bf16[2048,128]{1,0:T(8,128)(2,1)S(1)} %collective-permute-done.15.refs_2_) | copy-start | bytes 1572868
  156.1 32.3 %collective-permute-start.17 = (bf16[2048,128]{1,0:T(8,128)(2,1)S(1)}, bf16[2048,128]{1,0:T(8,128)(2,1)S(1)}, u32[]{:S(2)}, u32[]{:S(2)}) collective-permute-start(bf16[2048,128]{1,0:T(8,128)(2,1)S(1)} %collective-permute-done.15.refs_2_), channel_id=1, source_target_pairs={{0,1},{1,2},{2,3},{3,0},{4,5},{5,6},{6,7},{7,4},{8,9},{9,10},{10,1... | collective-permute-start | bytes 1572872 | tf_op jit(solution)/shard_map/ppermute | solution.py:321
  157.3 31.1 %copy-start.5 = (bf16[2576,128]{1,0:T(8,128)(2,1)}, bf16[2576,128]{1,0:T(8,128)(2,1)S(1)}, u32[]{:S(2)}) copy-start(bf16[2576,128]{1,0:T(8,128)(2,1)S(1)} %collective-permute-done.13.refs_7_.refs_17_.refs_21_.refs_25_.refs_29_) | copy-start | bytes 1978372
  157.3 40.9 %collective-permute-start.9 = (bf16[2048,128]{1,0:T(8,128)(2,1)}, bf16[2048,128]{1,0:T(8,128)(2,1)S(1)}, u32[]{:S(2)}, u32[]{:S(2)}) collective-permute-start(bf16[2048,128]{1,0:T(8,128)(2,1)} %pick.8.refs_1_), channel_id=1, source_target_pairs={{0,1},{1,2},{2,3},{3,0},{4,5},{5,6},{6,7},{7,4},{8,9},{9,10},{10,1... | collective-permute-start | bytes 1572872 | tf_op jit(solution)/shard_map/ppermute | solution.py:321
  176.0 22.2 %copy-start.14 = (bf16[2048,128]{1,0:T(8,128)(2,1)}, bf16[2048,128]{1,0:T(8,128)(2,1)S(1)}, u32[]{:S(2)}) copy-start(bf16[2048,128]{1,0:T(8,128)(2,1)S(1)} %collective-permute-done.10.refs_3_) | copy-start | bytes 1572868
  176.0 22.4 %collective-permute-start.11 = (bf16[2048,128]{1,0:T(8,128)(2,1)S(1)}, bf16[2048,128]{1,0:T(8,128)(2,1)S(1)}, u32[]{:S(2)}, u32[]{:S(2)}) collective-permute-start(bf16[2048,128]{1,0:T(8,128)(2,1)S(1)} %collective-permute-done.10.refs_3_), channel_id=1, source_target_pairs={{0,3},{1,0},{2,1},{3,2},{4,7},{5,4},{6,5},{7,6},{8,11},{9,8},{10,9... | collective-permute-start | bytes 1572872 | tf_op jit(solution)/shard_map/ppermute | solution.py:321
  182.1 6.3 %copy-start.9 = (bf16[2576,128]{1,0:T(8,128)(2,1)}, bf16[2576,128]{1,0:T(8,128)(2,1)S(1)}, u32[]{:S(2)}) copy-start(bf16[2576,128]{1,0:T(8,128)(2,1)S(1)} %collective-permute-done.14.refs_8_.refs_18_.refs_22_.refs_26_.refs_30_) | copy-start | bytes 1978372
  188.3 0.8 copy-start.26
  188.3 1.0 copy-start.30
  198.2 0.8 copy-start.20
  198.4 0.8 copy-start.23
  199.3 19.0 %copy-start.1 = (bf16[2576,128]{1,0:T(8,128)(2,1)S(1)}, bf16[2576,128]{1,0:T(8,128)(2,1)}, u32[]{:S(2)}) copy-start(bf16[2576,128]{1,0:T(8,128)(2,1)} %bundle.5.refs_5_.refs_15_.refs_19_.refs_23_.refs_27_) | copy-start | bytes 1978372
  214.3 21.2 %all-to-all-start.2 = ((bf16[32,128,128]{2,1,0:T(8,128)(2,1)}), bf16[32,128,128]{2,1,0:T(8,128)(2,1)S(1)}, u32[]{:S(2)}, u32[]{:S(2)}) async-start(bf16[32,128,128]{2,1,0:T(8,128)(2,1)} %get-tuple-element.42), calls=%async_computation.2 | async-start | bytes 2097152 | tf_op jit(solution)/shard_map/all_to_all | solution.py:334
  218.3 34.2 %collective-permute-start.21 = (bf16[2576,128]{1,0:T(8,128)(2,1)S(1)}, bf16[2576,128]{1,0:T(8,128)(2,1)S(1)}, u32[]{:S(2)}, u32[]{:S(2)}) collective-permute-start(bf16[2576,128]{1,0:T(8,128)(2,1)S(1)} %copy-done.1), channel_id=1, source_target_pairs={{0,1},{1,2},{2,3},{3,0},{4,5},{5,6},{6,7},{7,4},{8,9},{9,10},{10,1... | collective-permute-start | bytes 1978376 | tf_op jit(solution)/shard_map/ppermute | solution.py:321
  219.7 38.7 %collective-permute-start.22 = (bf16[2576,128]{1,0:T(8,128)(2,1)S(1)}, bf16[2576,128]{1,0:T(8,128)(2,1)S(1)}, u32[]{:S(2)}, u32[]{:S(2)}) collective-permute-start(bf16[2576,128]{1,0:T(8,128)(2,1)S(1)} %copy-done.1), channel_id=1, source_target_pairs={{0,3},{1,0},{2,1},{3,2},{4,7},{5,4},{6,5},{7,6},{8,11},{9,8},{10,9... | collective-permute-start | bytes 1978376 | tf_op jit(solution)/shard_map/ppermute | solution.py:321
  235.5 1.0 copy-start.13
  242.0 15.4 %collective-permute-start.24 = (bf16[2048,128]{1,0:T(8,128)(2,1)}, bf16[2048,128]{1,0:T(8,128)(2,1)S(1)}, u32[]{:S(2)}, u32[]{:S(2)}) collective-permute-start(bf16[2048,128]{1,0:T(8,128)(2,1)} %pick.11.refs_1_), channel_id=1, source_target_pairs={{0,1},{1,2},{2,3},{3,0},{4,5},{5,6},{6,7},{7,4},{8,9},{9,10},{10,1... | collective-permute-start | bytes 1572872 | tf_op jit(solution)/shard_map/ppermute | solution.py:321
  248.9 28.6 %collective-permute-start.19 = (bf16[2048,128]{1,0:T(8,128)(2,1)}, bf16[2048,128]{1,0:T(8,128)(2,1)S(1)}, u32[]{:S(2)}, u32[]{:S(2)}) collective-permute-start(bf16[2048,128]{1,0:T(8,128)(2,1)} %pick.10.refs_1_), channel_id=1, source_target_pairs={{0,3},{1,0},{2,1},{3,2},{4,7},{5,4},{6,5},{7,6},{8,11},{9,8},{10,9... | collective-permute-start | bytes 1572872 | tf_op jit(solution)/shard_map/ppermute | solution.py:321
  250.9 30.4 %collective-permute-start.23 = (bf16[2576,128]{1,0:T(8,128)(2,1)S(1)}, bf16[2576,128]{1,0:T(8,128)(2,1)S(1)}, u32[]{:S(2)}, u32[]{:S(2)}) collective-permute-start(bf16[2576,128]{1,0:T(8,128)(2,1)S(1)} %copy-done.1), channel_id=1, source_target_pairs={{0,2},{1,3},{2,0},{3,1},{4,6},{5,7},{6,4},{7,5},{8,10},{9,11},{10,... | collective-permute-start | bytes 1978376 | tf_op jit(solution)/shard_map/ppermute | solution.py:321
  252.5 36.9 %copy-start.6 = (bf16[2576,128]{1,0:T(8,128)(2,1)}, bf16[2576,128]{1,0:T(8,128)(2,1)S(1)}, u32[]{:S(2)}) copy-start(bf16[2576,128]{1,0:T(8,128)(2,1)S(1)} %collective-permute-done.21.refs_6_.refs_16_.refs_20_.refs_24_.refs_28_) | copy-start | bytes 1978372
  252.5 36.9 %collective-permute-start.25 = (bf16[2048,128]{1,0:T(8,128)(2,1)}, bf16[2048,128]{1,0:T(8,128)(2,1)S(1)}, u32[]{:S(2)}, u32[]{:S(2)}) collective-permute-start(bf16[2048,128]{1,0:T(8,128)(2,1)} %pick.11.refs_1_), channel_id=1, source_target_pairs={{0,3},{1,0},{2,1},{3,2},{4,7},{5,4},{6,5},{7,6},{8,11},{9,8},{10,9... | collective-permute-start | bytes 1572872 | tf_op jit(solution)/shard_map/ppermute | solution.py:321
  257.4 32.0 %copy-start.19 = (bf16[2048,128]{1,0:T(8,128)(2,1)}, bf16[2048,128]{1,0:T(8,128)(2,1)S(1)}, u32[]{:S(2)}) copy-start(bf16[2048,128]{1,0:T(8,128)(2,1)S(1)} %collective-permute-done.24.refs_2_) | copy-start | bytes 1572868
  257.4 32.0 %collective-permute-start.26 = (bf16[2048,128]{1,0:T(8,128)(2,1)S(1)}, bf16[2048,128]{1,0:T(8,128)(2,1)S(1)}, u32[]{:S(2)}, u32[]{:S(2)}) collective-permute-start(bf16[2048,128]{1,0:T(8,128)(2,1)S(1)} %collective-permute-done.24.refs_2_), channel_id=1, source_target_pairs={{0,1},{1,2},{2,3},{3,0},{4,5},{5,6},{6,7},{7,4},{8,9},{9,10},{10,1... | collective-permute-start | bytes 1572872 | tf_op jit(solution)/shard_map/ppermute | solution.py:321
  258.3 31.1 %copy-start.8 = (bf16[2576,128]{1,0:T(8,128)(2,1)}, bf16[2576,128]{1,0:T(8,128)(2,1)S(1)}, u32[]{:S(2)}) copy-start(bf16[2576,128]{1,0:T(8,128)(2,1)S(1)} %collective-permute-done.22.refs_7_.refs_17_.refs_21_.refs_25_.refs_29_) | copy-start | bytes 1978372
  258.3 40.9 %collective-permute-start.18 = (bf16[2048,128]{1,0:T(8,128)(2,1)}, bf16[2048,128]{1,0:T(8,128)(2,1)S(1)}, u32[]{:S(2)}, u32[]{:S(2)}) collective-permute-start(bf16[2048,128]{1,0:T(8,128)(2,1)} %pick.10.refs_1_), channel_id=1, source_target_pairs={{0,1},{1,2},{2,3},{3,0},{4,5},{5,6},{6,7},{7,4},{8,9},{9,10},{10,1... | collective-permute-start | bytes 1572872 | tf_op jit(solution)/shard_map/ppermute | solution.py:321
  277.5 22.0 %copy-start.16 = (bf16[2048,128]{1,0:T(8,128)(2,1)}, bf16[2048,128]{1,0:T(8,128)(2,1)S(1)}, u32[]{:S(2)}) copy-start(bf16[2048,128]{1,0:T(8,128)(2,1)S(1)} %collective-permute-done.19.refs_3_) | copy-start | bytes 1572868
  277.5 21.9 %collective-permute-start.20 = (bf16[2048,128]{1,0:T(8,128)(2,1)S(1)}, bf16[2048,128]{1,0:T(8,128)(2,1)S(1)}, u32[]{:S(2)}, u32[]{:S(2)}) collective-permute-start(bf16[2048,128]{1,0:T(8,128)(2,1)S(1)} %collective-permute-done.19.refs_3_), channel_id=1, source_target_pairs={{0,3},{1,0},{2,1},{3,2},{4,7},{5,4},{6,5},{7,6},{8,11},{9,8},{10,9... | collective-permute-start | bytes 1572872 | tf_op jit(solution)/shard_map/ppermute | solution.py:321
  281.2 8.1 %copy-start.11 = (bf16[2576,128]{1,0:T(8,128)(2,1)}, bf16[2576,128]{1,0:T(8,128)(2,1)S(1)}, u32[]{:S(2)}) copy-start(bf16[2576,128]{1,0:T(8,128)(2,1)S(1)} %collective-permute-done.23.refs_8_.refs_18_.refs_22_.refs_26_.refs_30_) | copy-start | bytes 1978372
  289.4 0.8 copy-start.28
  289.4 1.0 copy-start.31
  299.3 0.8 copy-start.22
  299.5 0.8 copy-start.27
